TPU v7x, 32 devices: a whole 2x2x4 slice. The times are simulated.
32 devices in a mesh: row: 8 (over z, x), col: 4 (over y, core).
Axes of the slice: x: 2, y: 2, z: 4, core: 2. Of those that a mesh axis runs over, the one named last changes fastest.
Arguments:
- vectors: bfloat16 [4, 4, 8, 16, 256], P(None, 'col', 'row'), may hold values from -6 to 6
- tiles: bfloat16 [8, 4, 64, 256, 256], P('row', 'col'), may hold values from -0.0625 to 0.0625
- tile_coords: int32 [8, 4, 64, 2], P('row', 'col'), may hold values from 0 to 127, as said below
- tile_count: int32 [8, 4], P('row', 'col'), may hold values from 16 to 64, as said below
Outputs:
- product: float32 [4, 4, 8, 16, 256], P(None, 'col', 'row')
Inputs may be any that keep to these rules, and one draw needn't show every extreme that they name: `tile_coords`: for the device in grid row r and grid column c every slot's block row I has I % 8 == r, its block column J has (J // 8) % 4 == c, and J <= I. `tile_count`: counts differ from device to device; in every draw some device uses all 64 slots and some other uses 64 // 4.
All inputs are finite; a program needn't handle non-finite values.
Results may differ from a plain program's by a relative error of at most 0.0003.
Values may be sent and summed in bfloat16 or wider, within the bound.
No kernel may reach another device: no remote copies, remote signals or barrier semaphores. Data moves between devices by JAX's collectives and lax.ppermute only.
A program may use at most 64 MiB of HBM per device.

v0:
```python
import jax
import jax.numpy as jnp
from jax import lax
from jax.sharding import PartitionSpec as P

TILE_GROUP = 8


def body(vectors, tiles, tile_coords, tile_count):
    grid_rows = lax.axis_size("row")
    grid_cols = lax.axis_size("col")
    repeats = vectors.shape[0]
    vec_count = vectors.shape[3]
    tile_width = vectors.shape[4]
    slot_count = tiles.shape[2]
    cells = grid_rows * grid_cols
    local_blocks = vectors.reshape(repeats, 1, vec_count, tile_width)
    column_blocks = lax.all_gather(local_blocks, "row", axis=1, tiled=True).reshape(
        repeats * grid_rows, vec_count, tile_width
    )
    row_blocks = lax.all_gather(local_blocks, "col", axis=1, tiled=True).reshape(
        repeats * grid_cols, vec_count, tile_width
    )
    matrices_all = tiles.reshape(slot_count, tile_width, tile_width)
    coords_all = tile_coords.reshape(slot_count, 2)
    filled = tile_count.reshape(())
    turns = (filled + TILE_GROUP - 1) // TILE_GROUP
    row_slots = jnp.arange(repeats * grid_cols, dtype=jnp.int32)
    col_slots = jnp.arange(repeats * grid_rows, dtype=jnp.int32)
    group_ids = jnp.arange(TILE_GROUP, dtype=jnp.int32)

    def load_group(turn):
        start = turn * TILE_GROUP
        matrices = lax.dynamic_slice_in_dim(matrices_all, start, TILE_GROUP, 0)
        positions = lax.dynamic_slice_in_dim(coords_all, start, TILE_GROUP, 0)
        active = start + group_ids < filled
        upper_index = positions[:, 0] // cells * grid_cols + positions[:, 0] % cells // grid_rows
        lower_index = positions[:, 1] // cells * grid_rows + positions[:, 1] % grid_rows
        row_hits = jnp.where(
            active[:, None] & (upper_index[:, None] == row_slots[None, :]), 1.0, 0.0
        ).astype(jnp.float32)
        col_hits = jnp.where(
            active[:, None] & (lower_index[:, None] == col_slots[None, :]), 1.0, 0.0
        ).astype(jnp.float32)
        return (matrices, upper_index, lower_index, row_hits, col_hits)

    def forward_add(total, matrices, lower_index, row_hits):
        sources = jnp.take(column_blocks, lower_index, axis=0)
        terms = jnp.einsum("snb,smb->snm", sources, matrices, preferred_element_type=jnp.float32)
        return total + jnp.einsum("su,snm->unm", row_hits, terms, precision=lax.Precision.HIGHEST)

    def mirror_add(total, matrices, upper_index, col_hits):
        targets = jnp.take(row_blocks, upper_index, axis=0)
        terms = jnp.einsum("snb,sbm->snm", targets, matrices, preferred_element_type=jnp.float32)
        return total + jnp.einsum("sv,snm->vnm", col_hits, terms, precision=lax.Precision.HIGHEST)

    row_start = jnp.zeros((repeats * grid_cols, vec_count, tile_width), jnp.float32)
    col_start = jnp.zeros((repeats * grid_rows, vec_count, tile_width), jnp.float32)

    def forward_turn(turn, total):
        matrices, upper_index, lower_index, row_hits, col_hits = load_group(turn)
        return forward_add(total, matrices, lower_index, row_hits)

    def mirror_turn(turn, total):
        matrices, upper_index, lower_index, row_hits, col_hits = load_group(turn)
        return mirror_add(total, matrices, upper_index, col_hits)

    row_acc = lax.fori_loop(0, turns, forward_turn, row_start)
    col_acc = lax.fori_loop(0, turns, mirror_turn, col_start)
    row_terms = row_acc.reshape(repeats, grid_cols, vec_count, tile_width)
    col_terms = col_acc.reshape(repeats, grid_rows, vec_count, tile_width)
    row_whole = lax.psum(row_terms, "col")
    col_whole = lax.psum(col_terms, "row")
    row_mine = lax.dynamic_slice_in_dim(row_whole, lax.axis_index("col"), 1, 1)
    col_mine = lax.dynamic_slice_in_dim(col_whole, lax.axis_index("row"), 1, 1)
    return (row_mine + col_mine).reshape(repeats, 1, 1, vec_count, tile_width)


def solution(mesh):
    return jax.shard_map(
        body,
        mesh=mesh,
        in_specs=(
            P(None, "col", "row", None, None),
            P("row", "col", None, None, None),
            P("row", "col", None, None),
            P("row", "col"),
        ),
        out_specs=P(None, "col", "row", None, None),
        check_vma=False,
    )
```

profile of v0, /device:TPU:0, one launch (start us, length us, event | category | flops | bytes accessed | tf_op | source)
XLA Modules:
  0.0 193.9 jit_solution(9262916242494318244)
XLA Ops:
  7.2 32.8 %all-gather = bf16[4,8,1,16,256]{4,3,2,1,0:T(8,128)(2,1)S(1)} all-gather(bf16[4,1,1,16,256]{4,3,2,1,0:T(8,128)(2,1)} %param.8), channel_id=2, replica_groups=mesh['row'=8,'col'=4] {'row'}, dimensions={1}, use_global_device_ids=true | all-gather | bytes 294912 | tf_op jit(solution)/shard_map/all_gather | solution.py:18
  40.0 16.9 %while.30 = (s32[]{:T(128)}, f32[16,16,256]{2,0,1:T(8,128)S(1)}, s32[]{:T(128)}, s32[]{:T(128)}, s32[64,2]{0,1:T(2,128)}, /*index=5*/bf16[32,16,256]{2,1,0:T(8,1...) while((s32[]{:T(128)}, f32[16,16,256]{2,0,1:T(8,128)S(1)}, ...), condition=%wide.region_1.2_spmd.clone, body=%wide.region_0.1_spmd.clone.sunk | while | flops 23168940 | bytes 2036267 | solution.py:68
  40.0 0.8 constant_dynamic-slice_fusion.4
  41.4 1.6 fusion.66
  44.3 0.8 constant_dynamic-slice_fusion.4
  45.6 1.6 fusion.66
  49.8 1.6 fusion.66
  54.0 1.6 fusion.66
  56.9 0.9 copy.5
  57.8 15.6 %all-gather.1 = bf16[4,4,1,16,256]{4,3,2,1,0:T(8,128)(2,1)S(1)} all-gather(bf16[4,1,1,16,256]{4,3,2,1,0:T(8,128)(2,1)S(1)} %copy-done), channel_id=3, replica_groups=mesh['row'=8,'col'=4] {'col'}, dimensions={1}, use_global_device_ids=true | all-gather | bytes 163840 | tf_op jit(solution)/shard_map/all_gather | solution.py:21
  73.5 17.5 %while.31 = (s32[]{:T(128)}, f32[32,16,256]{2,0,1:T(8,128)S(1)}, s32[]{:T(128)}, s32[]{:T(128)}, s32[64,2]{0,1:T(2,128)}, /*index=5*/bf16[16,16,256]{2,1,0:T(8,1...) while((s32[]{:T(128)}, f32[32,16,256]{2,0,1:T(8,128)S(1)}, ...), condition=%wide.region_4.5_spmd.clone, body=%wide.region_3.4_spmd.clone.sunk | while | flops 29526316 | bytes 2560555 | solution.py:69
  74.8 1.5 fusion.72
  77.0 0.8 convolution_add_fusion.5
  79.2 1.5 fusion.72
  81.4 0.8 convolution_add_fusion.5
  82.2 0.8 constant_dynamic-slice_fusion.5
  83.6 1.5 fusion.72
  85.8 0.8 convolution_add_fusion.5
  88.0 1.5 fusion.72
  90.2 0.8 convolution_add_fusion.5
  91.0 1.1 copy.6
  92.1 11.5 %all-reduce.3.cloned.1.call-done = f32[4,4,16,256]{3,2,1,0:T(8,128)} async-done(((f32[4,4,16,256]{3,2,1,0:T(8,128)}), f32[4,4,16,256]{3,2,1,0:T(8,128)}) %all-reduce.3.cloned.1.call-update) | async-done | bytes 262160 | tf_op jit(solution)/shard_map/psum | solution.py:72
  103.6 82.0 %all-reduce.5.cloned.1.call-done = f32[4,8,16,256]{3,2,1,0:T(8,128)} async-done(((f32[4,8,16,256]{3,2,1,0:T(8,128)}), f32[4,8,16,256]{3,2,1,0:T(8,128)}) %all-reduce.5.cloned.1.call-update) | async-done | bytes 524304 | tf_op jit(solution)/shard_map/psum | solution.py:73
  185.6 1.5 add_bitcast_fusion.1
  (57 shorter events, 16.1 us)
Async XLA Ops:
  6.5 51.3 %copy-start = (bf16[4,1,1,16,256]{4,3,2,1,0:T(8,128)(2,1)S(1)}, bf16[4,1,1,16,256]{4,3,2,1,0:T(8,128)(2,1)}, u32[]{:S(2)}) copy-start(bf16[4,1,1,16,256]{4,3,2,1,0:T(8,128)(2,1)} %param.8) | copy-start | bytes 98308
  6.5 97.1 %all-reduce.3.cloned.1.call-start = ((), (), s32[]{:S(2)}) async-start(), calls=%async_computation | async-start | bytes 524288 | tf_op jit(solution)/shard_map/psum | solution.py:72
  57.8 127.8 %all-reduce.5.cloned.1.call-start = ((), (), s32[]{:S(2)}) async-start(), calls=%async_computation.1 | async-start | bytes 1048576 | tf_op jit(solution)/shard_map/psum | solution.py:73
Sparse Core Ops, SparseCore 0:
  57.9 45.6 all-reduce.2
  107.0 78.5 all-reduce.4
where the time goes:
time: 195 us; the launch traced here: 194 us
  waiting for transfers between devices  93.5 us (48%)
  blocking collectives  48.3 us (25%)
  matrix products  17.8 us (9%)
  between operations  14.1 us (7%)
  local copies, waits for them, and re-layouts  12.5 us (6%)
  other arithmetic  7.16 us (4%)
    psum x1, waiting for transfers between devices, body(): col_whole = lax.psum(col_terms, 'row')  82 us
    all_gather x1, blocking collectives, body(): lax.all_gather(local_blocks, 'row', axis=1, tiled=True)  32.8 us
    all_gather x1, blocking collectives, body(): lax.all_gather(local_blocks, 'col', axis=1, tiled=True)  15.6 us
    psum x1, waiting for transfers between devices, body(): row_whole = lax.psum(row_terms, 'col')  11.5 us
    dot_general x4, matrix products, forward_add(): jnp.einsum('snb,smb->snm', sources, matrices, preferred_element_type=jnp....  6.44 us
    dot_general x4, matrix products, mirror_add(): jnp.einsum('snb,sbm->snm', targets, matrices, preferred_element_type=jnp....  6.05 us
    dynamic_slice x8, local copies, waits for them, and re-layouts, load_group(): positions = lax.dynamic_slice_in_dim(coords_all, start, TILE_GROUP, 0)  6.04 us
    lt x8, other arithmetic, load_group(): active = start + group_ids < filled  5.23 us
  transfers between devices with their start and end apart: 2, of which 2 were waited for; matrix products, arithmetic and copies ran while one was open for 9% of the time, Pallas kernels for 0%

commit v1 on v0

--- a/solution.py
+++ b/solution.py
@@ -15,9 +15,9 @@
     slot_count = tiles.shape[2]
     cells = grid_rows * grid_cols
     local_blocks = vectors.reshape(repeats, 1, vec_count, tile_width)
-    column_blocks = lax.all_gather(local_blocks, "row", axis=1, tiled=True).reshape(
-        repeats * grid_rows, vec_count, tile_width
-    )
+    column_blocks = jnp.concatenate(
+        lax.all_to_all(jnp.stack([local_blocks] * lax.axis_size("row")), "row", 0, 0), axis=1
+    ).reshape(repeats * grid_rows, vec_count, tile_width)
     row_blocks = lax.all_gather(local_blocks, "col", axis=1, tiled=True).reshape(
         repeats * grid_cols, vec_count, tile_width
     )

time: 195 us -> 174 us (0.89)
  blocking collectives: 48.3 us -> 5.63 us
  waiting for transfers between devices: 93.5 us -> 106 us
  starting transfers between devices: 0.04 us -> 7.36 us
    all_gather x1 -> x0, blocking collectives: 32.8 us -> none  [body(): lax.all_gather(local_blocks, 'row', axis=1, tiled=True)]
    psum x1, waiting for transfers between devices: 11.5 us -> 33.8 us  [body(): row_whole = lax.psum(row_terms, 'col')]
    all_gather x1, blocking collectives: 15.6 us -> 5.63 us  [body(): lax.all_gather(local_blocks, 'col', axis=1, tiled=True)]
    psum x1, waiting for transfers between devices: 82 us -> 72 us  [body(): col_whole = lax.psum(col_terms, 'row')]
    all_to_all x0 -> x1, starting transfers between devices: none -> 7.28 us  [body(): lax.all_to_all(jnp.stack([local_blocks] * lax.axis_size('row')), 'row', 0...]
  transfers between devices with their start and end apart: 2 -> 3, of which waited for: 2 -> 2; matrix products, arithmetic and copies ran while one was open for 9% -> 21% of each run, Pallas kernels for 0% -> 0%
where the time goes in v1:
time: 174 us; the launch traced here: 172 us
  waiting for transfers between devices  106 us (61%)
  matrix products  17.8 us (10%)
  between operations  14.1 us (8%)
  local copies, waits for them, and re-layouts  14 us (8%)
  starting transfers between devices  7.36 us (4%)
  other arithmetic  7.16 us (4%)
  blocking collectives  5.63 us (3%)
    psum x1, waiting for transfers between devices, body(): col_whole = lax.psum(col_terms, 'row')  72 us
    psum x1, waiting for transfers between devices, body(): row_whole = lax.psum(row_terms, 'col')  33.8 us
    all_to_all x1, starting transfers between devices, body(): lax.all_to_all(jnp.stack([local_blocks] * lax.axis_size('row')), 'row', 0...  7.28 us
    dot_general x4, matrix products, forward_add(): jnp.einsum('snb,smb->snm', sources, matrices, preferred_element_type=jnp....  6.44 us
    dot_general x4, matrix products, mirror_add(): jnp.einsum('snb,sbm->snm', targets, matrices, preferred_element_type=jnp....  6.04 us
    dynamic_slice x8, local copies, waits for them, and re-layouts, load_group(): positions = lax.dynamic_slice_in_dim(coords_all, start, TILE_GROUP, 0)  6.04 us
    all_gather x1, blocking collectives, body(): lax.all_gather(local_blocks, 'col', axis=1, tiled=True)  5.63 us
    lt x8, other arithmetic, load_group(): active = start + group_ids < filled  5.23 us
  transfers between devices with their start and end apart: 3, of which 2 were waited for; matrix products, arithmetic and copies ran while one was open for 21% of the time, Pallas kernels for 0%

profile of v1, /device:TPU:0, one launch (start us, length us, event | category | flops | bytes accessed | tf_op | source)
XLA Modules:
  0.0 172.4 jit_solution(2892209236763014326)
XLA Ops:
  6.5 1.5 stack.3
  8.0 7.3 %all-to-all-start = ((bf16[8,4,1,16,256]{4,3,1,2,0:T(8,128)(2,1)}), bf16[8,4,1,16,256]{4,3,1,2,0:T(8,128)(2,1)S(1)}, u32[]{:S(2)}, u32[]{:S(2)}) async-start(bf16[8,4,1,16,256]{4,3,1,2,0:T(8,128)(2,1)} %stack.3), calls=%async_computation | async-start | bytes 524288 | tf_op jit(solution)/shard_map/all_to_all | solution.py:19
  16.0 5.6 %all-gather = bf16[4,4,1,16,256]{4,3,2,1,0:T(8,128)(2,1)S(1)} all-gather(bf16[4,1,1,16,256]{4,3,2,1,0:T(8,128)(2,1)} %param.8), channel_id=2, replica_groups=mesh['row'=8,'col'=4] {'col'}, dimensions={1}, use_global_device_ids=true | all-gather | bytes 163840 | tf_op jit(solution)/shard_map/all_gather | solution.py:21
  21.7 17.5 %while.31 = (s32[]{:T(128)}, f32[32,16,256]{2,0,1:T(8,128)S(1)}, s32[]{:T(128)}, s32[]{:T(128)}, s32[64,2]{0,1:T(2,128)}, /*index=5*/bf16[16,16,256]{2,1,0:T(8,1...) while((s32[]{:T(128)}, f32[32,16,256]{2,0,1:T(8,128)S(1)}, ...), condition=%wide.region_4.5_spmd.clone, body=%wide.region_3.4_spmd.clone.sunk | while | flops 29526316 | bytes 2560555 | solution.py:69
  21.7 0.8 constant_dynamic-slice_fusion.5
  23.1 1.5 fusion.72
  25.3 0.8 convolution_add_fusion.5
  26.1 0.8 constant_dynamic-slice_fusion.5
  27.4 1.5 fusion.72
  29.6 0.8 convolution_add_fusion.5
  31.8 1.5 fusion.72
  34.0 0.8 convolution_add_fusion.5
  36.2 1.5 fusion.72
  38.4 0.8 convolution_add_fusion.5
  39.2 1.1 copy.17
  40.4 16.9 %while.30 = (s32[]{:T(128)}, f32[16,16,256]{2,0,1:T(8,128)S(1)}, s32[]{:T(128)}, s32[]{:T(128)}, s32[64,2]{0,1:T(2,128)}, /*index=5*/bf16[32,16,256]{2,1,0:T(8,1...) while((s32[]{:T(128)}, f32[16,16,256]{2,0,1:T(8,128)S(1)}, ...), condition=%wide.region_1.2_spmd.clone, body=%wide.region_0.1_spmd.clone.sunk | while | flops 23168940 | bytes 2036267 | solution.py:68
  41.8 1.6 fusion.66
  46.0 1.6 fusion.66
  50.2 1.6 fusion.66
  54.4 1.6 fusion.66
  57.3 0.9 copy.16
  58.2 72.0 %all-reduce.5.cloned.1.call-done = f32[4,8,16,256]{3,2,1,0:T(8,128)} async-done(((f32[4,8,16,256]{3,2,1,0:T(8,128)}), f32[4,8,16,256]{3,2,1,0:T(8,128)}) %all-reduce.5.cloned.1.call-update) | async-done | bytes 524304 | tf_op jit(solution)/shard_map/psum | solution.py:73
  130.2 33.8 %all-reduce.3.cloned.1.call-done = f32[4,4,16,256]{3,2,1,0:T(8,128)} async-done(((f32[4,4,16,256]{3,2,1,0:T(8,128)}), f32[4,4,16,256]{3,2,1,0:T(8,128)}) %all-reduce.3.cloned.1.call-update) | async-done | bytes 262160 | tf_op jit(solution)/shard_map/psum | solution.py:72
  164.1 1.5 add_bitcast_fusion.1
  (58 shorter events, 16.9 us)
Async XLA Ops:
  8.0 32.3 %all-to-all-start = ((bf16[8,4,1,16,256]{4,3,1,2,0:T(8,128)(2,1)}), bf16[8,4,1,16,256]{4,3,1,2,0:T(8,128)(2,1)S(1)}, u32[]{:S(2)}, u32[]{:S(2)}) async-start(bf16[8,4,1,16,256]{4,3,1,2,0:T(8,128)(2,1)} %stack.3), calls=%async_computation | async-start | bytes 524288 | tf_op jit(solution)/shard_map/all_to_all | solution.py:19
  15.3 114.9 %all-reduce.5.cloned.1.call-start = ((), (), s32[]{:S(2)}) async-start(), calls=%async_computation.2 | async-start | bytes 1048576 | tf_op jit(solution)/shard_map/psum | solution.py:73
  40.3 123.8 %all-reduce.3.cloned.1.call-start = ((), (), s32[]{:S(2)}) async-start(), calls=%async_computation.1 | async-start | bytes 524288 | tf_op jit(solution)/shard_map/psum | solution.py:72
Sparse Core Ops, SparseCore 0:
  40.4 89.7 all-reduce.4
  132.5 31.4 all-reduce.2
